TPU v7x, 512 devices: a whole 4x8x8 slice. The times are simulated.
512 devices in a mesh: seq: 32 (over x, y), dp: 8 (over z), domain: 2 (over core).
Axes of the slice: x: 4, y: 8, z: 8, core: 2. Of those that a mesh axis runs over, the one named last changes fastest.
Arguments:
- history: bfloat16 [2, 8, 8192, 1024], P('domain', 'dp', 'seq'), may hold values from -6 to 6
- qkv_weight: bfloat16 [2, 1024, 3072], P('domain', 'seq'), may hold values from -0.375 to 0.375
- norm_gain: float32 [2, 1024], P('domain'), may hold values from 0.1 to 1.9
- pool_gain: float32 [2, 1024], P('domain'), may hold values from 0.1 to 1.9
- lengths: int32 [2, 8], P('domain', 'dp'), may hold values from 1024 to 8192, as said below
- positives: int32 [8], replicated, may hold values from 0 to 7, each once
Outputs:
- user_vec: bfloat16 [2, 8, 1024], P('domain', 'dp', 'seq')
- loss: float32 [2, 8], P('domain', 'dp')
Inputs may be any that keep to these rules, and one draw needn't show every extreme that they name: `lengths`: in each domain one user has exactly 8192 valid events and another exactly 1024. `positives`: each user of the second domain is named exactly once.
All inputs are finite; a program needn't handle non-finite values.
Results may differ from a plain program's by a relative error of at most 0.0085.
Values may be sent and summed in bfloat16 or wider, within the bound.
A program may use at most 64 MiB of HBM per device.

v0:
```python
import jax
import jax.numpy as jnp
from jax import lax
from jax.sharding import PartitionSpec as P

HEADS = 8
HEAD_DIM = 128
logit_scale = 20.0
epsilon = 1e-06
highest = lax.Precision.HIGHEST


def carried_in(part, axis, combine, identity):
    place = lax.axis_index(axis)
    gathered = jax.tree.map(lambda a: lax.all_gather(a, axis), part)
    state = jax.tree.map(lambda a, e: jnp.zeros_like(a) + jnp.asarray(e, a.dtype), part, identity)

    def one(hop, state):
        return combine(
            state, jax.tree.map(lambda a: lax.dynamic_index_in_dim(a, hop, 0, False), gathered)
        )

    return lax.fori_loop(0, place, one, state)


def partner_2(block, axis, stride):
    count = lax.axis_size(axis)
    route = []
    for low in range(count):
        high = low | 1 << stride
        if high != low and high < count:
            route += [(low, high), (high, low)]
    return lax.ppermute(block, axis, route)


def feature_map(values):
    return jax.nn.elu(values) + 1.0


def add_pair(earlier, later):
    return (earlier[0] + later[0], earlier[1] + later[1])


def shards(history, qkv_weight, norm_gain, pool_gain, lengths, positives):
    seq_count = lax.axis_size("seq")
    seq_place = lax.axis_index("seq")
    group_place = lax.axis_index("dp")
    domain_place = lax.axis_index("domain")
    events = history[0]
    users_dev, tokens_dev, width = events.shape
    row_count = users_dev * tokens_dev
    wide = events.astype(jnp.float32)
    normed = (
        wide * lax.rsqrt(jnp.mean(wide * wide, -1, keepdims=True) + epsilon) * norm_gain[0]
    ).astype(jnp.bfloat16)
    normed = normed.reshape(row_count, width)
    rows_here = qkv_weight[0]

    def add_rows(piece):
        return jnp.dot(normed, piece, preferred_element_type=jnp.float32)

    query_raw = add_rows(lax.all_gather(rows_here[:, :width], "seq", axis=0, tiled=True))
    key_raw = add_rows(lax.all_gather(rows_here[:, width : 2 * width], "seq", axis=0, tiled=True))
    value_raw = add_rows(lax.all_gather(rows_here[:, 2 * width :], "seq", axis=0, tiled=True))
    positions = seq_place * tokens_dev + jnp.arange(tokens_dev)
    valid = positions[None, :] < lengths[0][:, None]
    shape_heads = (users_dev, tokens_dev, HEADS, HEAD_DIM)
    queries = feature_map(query_raw).astype(jnp.bfloat16).reshape(shape_heads)
    key_feats = (
        jnp.where(valid.reshape(row_count)[:, None], feature_map(key_raw), 0.0)
        .astype(jnp.bfloat16)
        .reshape(shape_heads)
    )
    val_feats = value_raw.astype(jnp.bfloat16).reshape(shape_heads)
    local_state = jnp.einsum(
        "uthc,uthd->uhcd", key_feats, val_feats, preferred_element_type=jnp.float32
    )
    local_total = jnp.sum(key_feats.astype(jnp.float32), axis=1)
    state_before, total_before = carried_in(
        (local_state, local_total),
        "seq",
        add_pair,
        (jnp.zeros_like(local_state), jnp.zeros_like(local_total)),
    )
    causal = jnp.arange(tokens_dev)[:, None] >= jnp.arange(tokens_dev)[None, :]
    scores = jnp.einsum("uthc,ushc->uhts", queries, key_feats, preferred_element_type=jnp.float32)
    scores = jnp.where(causal, scores, 0.0)
    denominator = jnp.sum(scores, axis=-1) + jnp.einsum(
        "uthc,uhc->uht", queries.astype(jnp.float32), total_before, precision=highest
    )
    numerator = jnp.einsum(
        "uhts,ushc->uthc",
        scores.astype(jnp.bfloat16),
        val_feats,
        preferred_element_type=jnp.float32,
    )
    numerator = numerator + jnp.einsum(
        "uthc,uhcd->uthd",
        queries,
        state_before.astype(jnp.bfloat16),
        preferred_element_type=jnp.float32,
    )
    attended = numerator / jnp.transpose(denominator, (0, 2, 1))[..., None]
    attended = attended.reshape(users_dev, tokens_dev, width)
    partial_value = jnp.sum(jnp.where(valid[..., None], wide + attended, 0.0), axis=1)
    piece_width = width // seq_count
    gain_row = pool_gain[0]
    pooled = lax.psum(partial_value, "seq")
    factor = lax.rsqrt(jnp.mean(pooled * pooled, -1, keepdims=True) + epsilon)
    full_vec = (pooled * factor * gain_row).astype(jnp.bfloat16)
    out_vec = lax.dynamic_slice_in_dim(full_vec, seq_place * piece_width, piece_width, 1)
    group = lax.all_gather(full_vec, "dp", axis=0, tiled=True)
    other = partner_2(group, "domain", 0)
    logits = jnp.einsum("uc,vc->uv", full_vec, other, preferred_element_type=jnp.float32) * (
        logit_scale / width
    )
    users_all = other.shape[0]
    own_index = group_place * users_dev + jnp.arange(users_dev)
    targets = lax.dynamic_slice_in_dim(positives, group_place * users_dev, users_dev)
    forward_pair = targets[:, None] == jnp.arange(users_all)[None, :]
    backward_pair = positives[None, :] == own_index[:, None]
    partner = jnp.where(domain_place == 0, forward_pair, backward_pair)
    loss = jnp.log(jnp.sum(jnp.exp(logits), axis=-1)) - jnp.sum(
        jnp.where(partner, logits, 0.0), axis=-1
    )
    return (out_vec[None], loss[None])


def solution(mesh):
    placed = (
        P("domain", "dp", "seq", None),
        P("domain", "seq", None),
        P("domain", None),
        P("domain", None),
        P("domain", "dp"),
        P(),
    )
    return jax.shard_map(
        shards,
        mesh=mesh,
        in_specs=placed,
        out_specs=(P("domain", "dp", "seq"), P("domain", "dp")),
        check_vma=False,
    )
```

profile of v0, /device:TPU:1, one launch (start us, length us, event | category | flops | bytes accessed | tf_op | source)
XLA Modules:
  0.0 566.4 jit_solution(12575679889314143297)
XLA Ops:
  7.2 0.0 all-gather.11.cloned.1.call-start
  7.2 1.6 fusion.51
  8.8 0.0 all-gather.11.cloned.1.call-update
  8.8 0.0 all-gather.7.cloned.1.call-start
  8.9 0.7 all-gather.7.cloned.1.call-update
  9.6 0.0 all-gather.9.cloned.1.call-start
  9.6 0.7 all-gather.9.cloned.1.call-update
  10.3 0.0 all-gather.13.cloned.1.call-start
  11.0 1.2 fusion.5
  12.2 82.9 %all-gather.11.cloned.1.call-done = bf16[1024,1024]{1,0:T(8,128)(2,1)} async-done(((bf16[32,1024]{1,0:T(8,128)(2,1)}), bf16[1024,1024]{1,0:T(8,128)(2,1)}) %all-gather.11.cloned.1.call-update) | async-done | bytes 2097168 | tf_op jit(solution)/shard_map/all_gather | solution.py:63
  95.1 0.0 copy-start
  95.1 0.0 copy-start.2
  95.1 3.0 convert_reduce_fusion
  98.1 0.2 copy.43
  98.3 0.0 copy-start.3
  98.3 80.6 %all-gather.7.cloned.1.call-done = bf16[1024,1024]{1,0:T(8,128)(2,1)} async-done(((bf16[32,1024]{1,0:T(8,128)(2,1)}), bf16[1024,1024]{1,0:T(8,128)(2,1)}) %all-gather.7.cloned.1.call-update) | async-done | bytes 2097168 | tf_op jit(solution)/shard_map/all_gather | solution.py:64
  178.9 0.0 copy-done
  178.9 0.0 copy-done.2
  178.9 2.4 fusion.3
  181.3 1.1 fusion.29
  182.4 0.0 all-gather.13.cloned.1.call-update
  182.4 0.0 copy-done.3
  182.4 0.7 dynamic_slice.15
  183.1 31.5 %all_gather.30 = f32[32,1,8,128]{3,2,1,0:T(8,128)S(1)} all-gather(f32[1,1,8,128]{3,2,1,0:T(8,128)S(1)} %bitcast.122), channel_id=1, replica_groups=mesh['seq'=32,'dp'=8,'domain'=2] {'seq'}, dimensions={0}, use_global_device_ids=true | all-gather | bytes 135168 | tf_op jit(solution)/shard_map/all_gather | solution.py:15
  214.6 48.1 %all-gather.9.cloned.1.call-done = bf16[1024,1024]{1,0:T(8,128)(2,1)} async-done(((bf16[32,1024]{1,0:T(8,128)(2,1)}), bf16[1024,1024]{1,0:T(8,128)(2,1)}) %all-gather.9.cloned.1.call-update) | async-done | bytes 2097168 | tf_op jit(solution)/shard_map/all_gather | solution.py:62
  262.7 2.7 fusion.22
  265.4 0.0 copy-start.4
  265.4 0.5 select_reduce_fusion
  266.0 0.4 fusion.11
  266.3 145.7 %all-gather.13.cloned.1.call-done = f32[256,128,128]{2,1,0:T(8,128)} async-done(((f32[8,128,128]{2,1,0:T(8,128)}), f32[256,128,128]{2,1,0:T(8,128)}) %all-gather.13.cloned.1.call-update) | async-done | bytes 16777232 | tf_op jit(solution)/shard_map/all_gather | solution.py:15
  412.1 0.0 copy-done.4
  412.1 0.5 fusion.24
  412.6 1.4 fusion.21
  414.0 0.0 copy-start.1
  414.0 0.3 copy.37
  414.3 0.2 fusion.7
  414.6 94.9 %psum.7 = f32[1,1024]{1,0:T(1,128)S(1)} all-reduce(f32[1,1024]{1,0:T(1,128)S(1)} %bitcast.119), channel_id=1, replica_groups=mesh['seq'=32,'dp'=8,'domain'=2] {'seq'}, use_global_device_ids=true, to_apply=%region_6.7 | all-reduce | flops 1024 | bytes 8192 | tf_op jit(solution)/shard_map/psum | solution.py:108
  509.5 0.6 multiply_reduce_fusion
  510.8 0.0 copy-done.1
  510.8 20.9 %all-gather.1 = bf16[8,1,1024]{2,1,0:T(2,128)(2,1)S(1)} all-gather(bf16[1,1,1024]{2,1,0:T(2,128)(2,1)S(1)} %bitcast.121), channel_id=1, replica_groups=mesh['seq'=32,'dp'=8,'domain'=2] {'dp'}, dimensions={0}, use_global_device_ids=true | all-gather | bytes 18432 | tf_op jit(solution)/shard_map/all_gather | solution.py:112
  531.7 23.3 %collective-permute-start = (bf16[8,1024]{1,0:T(8,128)(2,1)S(1)}, bf16[8,1024]{1,0:T(8,128)(2,1)S(1)}, u32[]{:S(2)}, u32[]{:S(2)}) collective-permute-start(bf16[8,1024]{1,0:T(8,128)(2,1)S(1)} %bitcast.120), channel_id=1, source_target_pairs={{0,1},{1,0},{2,3},{3,2},{4,5},{5,4},{6,7},{7,6},{8,9},{9,8},{10,11... | collective-permute-start | bytes 49160 | tf_op jit(solution)/shard_map/ppermute | solution.py:33
  555.0 0.6 dynamic-slice_bitcast_fusion
  555.6 0.2 collective-permute-done
  555.8 1.5 fusion.40
  (9 shorter events, 0.1 us)
Async XLA Ops:
  7.2 87.9 %all-gather.11.cloned.1.call-start = ((), (), s32[]{:S(2)}) async-start(), calls=%async_computation.2 | async-start | bytes 2162688 | tf_op jit(solution)/shard_map/all_gather | solution.py:63
  8.8 170.1 %all-gather.7.cloned.1.call-start = ((), (), s32[]{:S(2)}) async-start(), calls=%async_computation | async-start | bytes 2162688 | tf_op jit(solution)/shard_map/all_gather | solution.py:64
  9.6 253.1 %all-gather.9.cloned.1.call-start = ((), (), s32[]{:S(2)}) async-start(), calls=%async_computation.1 | async-start | bytes 2162688 | tf_op jit(solution)/shard_map/all_gather | solution.py:62
  10.3 401.7 %all-gather.13.cloned.1.call-start = ((), (), s32[]{:S(2)}) async-start(), calls=%async_computation.3 | async-start | bytes 17301504 | tf_op jit(solution)/shard_map/all_gather | solution.py:15
  95.1 83.8 %copy-start = (bf16[1,1,256,1024]{3,2,1,0:T(8,128)(2,1)S(1)}, bf16[1,1,256,1024]{3,2,1,0:T(8,128)(2,1)}, u32[]{:S(2)}) copy-start(bf16[1,1,256,1024]{3,2,1,0:T(8,128)(2,1)} %param.8) | copy-start | bytes 1572868
  95.1 83.8 %copy-start.2 = (f32[1,1024]{1,0:T(1,128)S(1)}, f32[1,1024]{1,0:T(1,128)}, u32[]{:S(2)}) copy-start(f32[1,1024]{1,0:T(1,128)} %param.10) | copy-start | bytes 12292
  98.3 84.1 %copy-start.3 = (s32[8]{0:T(128)S(1)}, s32[8]{0:T(128)}, u32[]{:S(2)}) copy-start(s32[8]{0:T(128)} %param.13) | copy-start | bytes 100
  265.4 146.6 %copy-start.4 = (bf16[32,8,8,128]{3,2,1,0:T(8,128)(2,1)}, bf16[32,8,8,128]{3,2,1,0:T(8,128)(2,1)S(1)}, u32[]{:S(2)}) copy-start(bf16[32,8,8,128]{3,2,1,0:T(8,128)(2,1)S(1)} %fusion.22) | copy-start | bytes 1572868
  414.0 96.8 %copy-start.1 = (f32[1,1024]{1,0:T(1,128)S(1)}, f32[1,1024]{1,0:T(1,128)}, u32[]{:S(2)}) copy-start(f32[1,1024]{1,0:T(1,128)} %param.11) | copy-start | bytes 12292
  531.7 24.1 %collective-permute-start = (bf16[8,1024]{1,0:T(8,128)(2,1)S(1)}, bf16[8,1024]{1,0:T(8,128)(2,1)S(1)}, u32[]{:S(2)}, u32[]{:S(2)}) collective-permute-start(bf16[8,1024]{1,0:T(8,128)(2,1)S(1)} %bitcast.120), channel_id=1, source_target_pairs={{0,1},{1,0},{2,3},{3,2},{4,5},{5,4},{6,7},{7,6},{8,9},{9,8},{10,11... | collective-permute-start | bytes 49160 | tf_op jit(solution)/shard_map/ppermute | solution.py:33
Sparse Core Ops, SparseCore 0:
  11.1 83.9 all-gather.10
  98.3 80.6 all-gather.6
  182.1 80.5 all-gather.8
  265.7 146.2 all-gather.12
where the time goes:
time: 568 us; the launch traced here: 566 us
  waiting for transfers between devices  359 us (63%)
  blocking collectives  147 us (26%)
  starting transfers between devices  23.4 us (4%)
  between operations  17.8 us (3%)
  matrix products  13.5 us (2%)
    all_gather x1, waiting for transfers between devices, carried_in(): gathered = jax.tree.map(lambda a: lax.all_gather(a, axis), part)  146 us
    psum x1, blocking collectives, shards(): pooled = lax.psum(partial_value, 'seq')  94.9 us
    all_gather x1, waiting for transfers between devices, shards(): lax.all_gather(rows_here[:, width:2 * width], 'seq', axis=0, tiled=True)  82.9 us
    all_gather x1, waiting for transfers between devices, shards(): lax.all_gather(rows_here[:, 2 * width:], 'seq', axis=0, tiled=True)  80.6 us
    all_gather x1, waiting for transfers between devices, shards(): lax.all_gather(rows_here[:, :width], 'seq', axis=0, tiled=True)  48.1 us
    all_gather x1, blocking collectives, carried_in(): gathered = jax.tree.map(lambda a: lax.all_gather(a, axis), part)  31.5 us
    ppermute x1, starting transfers between devices, partner_2(): return lax.ppermute(block, axis, route)  23.3 us
    all_gather x1, blocking collectives, shards(): group = lax.all_gather(full_vec, 'dp', axis=0, tiled=True)  20.9 us
  transfers between devices with their start and end apart: 5, of which 5 were waited for; matrix products, arithmetic and copies ran while one was open for 2% of the time, Pallas kernels for 0%

commit v1 on v0

--- a/solution.py
+++ b/solution.py
@@ -105,7 +105,7 @@
     partial_value = jnp.sum(jnp.where(valid[..., None], wide + attended, 0.0), axis=1)
     piece_width = width // seq_count
     gain_row = pool_gain[0]
-    pooled = lax.psum(partial_value, "seq")
+    pooled = jnp.sum(lax.all_gather(partial_value, "seq"), axis=0)
     factor = lax.rsqrt(jnp.mean(pooled * pooled, -1, keepdims=True) + epsilon)
     full_vec = (pooled * factor * gain_row).astype(jnp.bfloat16)
     out_vec = lax.dynamic_slice_in_dim(full_vec, seq_place * piece_width, piece_width, 1)

time: 568 us -> 533 us (0.938)
  blocking collectives: 147 us -> 117 us
    psum x1 -> x0, blocking collectives: 94.9 us -> none  [shards(): pooled = lax.psum(partial_value, 'seq')]
    all_gather x0 -> x1, blocking collectives: none -> 65.2 us  [shards(): pooled = jnp.sum(lax.all_gather(partial_value, 'seq'), axis=0)]
where the time goes in v1:
time: 533 us; the launch traced here: 531 us
  waiting for transfers between devices  359 us (67%)
  blocking collectives  117 us (22%)
  starting transfers between devices  18.2 us (3%)
  between operations  17.8 us (3%)
  matrix products  13.5 us (3%)
    all_gather x1, waiting for transfers between devices, carried_in(): gathered = jax.tree.map(lambda a: lax.all_gather(a, axis), part)  146 us
    all_gather x1, waiting for transfers between devices, shards(): lax.all_gather(rows_here[:, width:2 * width], 'seq', axis=0, tiled=True)  82.9 us
    all_gather x1, waiting for transfers between devices, shards(): lax.all_gather(rows_here[:, 2 * width:], 'seq', axis=0, tiled=True)  80.6 us
    all_gather x1, blocking collectives, shards(): pooled = jnp.sum(lax.all_gather(partial_value, 'seq'), axis=0)  65.2 us
    all_gather x1, waiting for transfers between devices, shards(): lax.all_gather(rows_here[:, :width], 'seq', axis=0, tiled=True)  48.1 us
    all_gather x1, blocking collectives, carried_in(): gathered = jax.tree.map(lambda a: lax.all_gather(a, axis), part)  31.5 us
    all_gather x1, blocking collectives, shards(): group = lax.all_gather(full_vec, 'dp', axis=0, tiled=True)  20.5 us
    ppermute x1, starting transfers between devices, partner_2(): return lax.ppermute(block, axis, route)  18 us
  transfers between devices with their start and end apart: 5, of which 5 were waited for; matrix products, arithmetic and copies ran while one was open for 2% of the time, Pallas kernels for 0%

profile of v1, /device:TPU:1, one launch (start us, length us, event | category | flops | bytes accessed | tf_op | source)
XLA Modules:
  0.0 531.1 jit_solution(3756560640286931976)
XLA Ops:
  7.2 0.0 all-gather.12.cloned.1.call-start
  7.2 1.6 fusion.51
  8.8 0.0 all-gather.12.cloned.1.call-update
  8.8 0.0 all-gather.8.cloned.1.call-start
  8.9 0.7 all-gather.8.cloned.1.call-update
  9.6 0.0 all-gather.10.cloned.1.call-start
  9.6 0.7 all-gather.10.cloned.1.call-update
  10.3 0.0 all-gather.14.cloned.1.call-start
  11.0 1.2 fusion.5
  12.2 82.9 %all-gather.12.cloned.1.call-done = bf16[1024,1024]{1,0:T(8,128)(2,1)} async-done(((bf16[32,1024]{1,0:T(8,128)(2,1)}), bf16[1024,1024]{1,0:T(8,128)(2,1)}) %all-gather.12.cloned.1.call-update) | async-done | bytes 2097168 | tf_op jit(solution)/shard_map/all_gather | solution.py:63
  95.1 0.0 copy-start
  95.1 0.0 copy-start.2
  95.1 3.0 convert_reduce_fusion
  98.1 0.2 copy.53
  98.3 0.0 copy-start.3
  98.3 80.6 %all-gather.8.cloned.1.call-done = bf16[1024,1024]{1,0:T(8,128)(2,1)} async-done(((bf16[32,1024]{1,0:T(8,128)(2,1)}), bf16[1024,1024]{1,0:T(8,128)(2,1)}) %all-gather.8.cloned.1.call-update) | async-done | bytes 2097168 | tf_op jit(solution)/shard_map/all_gather | solution.py:64
  178.9 0.0 copy-done
  178.9 0.0 copy-done.2
  178.9 2.4 fusion.3
  181.3 1.1 fusion.29
  182.4 0.0 all-gather.14.cloned.1.call-update
  182.4 0.0 copy-done.3
  182.4 0.7 dynamic_slice.15
  183.1 31.5 %all_gather.36 = f32[32,1,8,128]{3,2,1,0:T(8,128)S(1)} all-gather(f32[1,1,8,128]{3,2,1,0:T(8,128)S(1)} %bitcast.122), channel_id=1, replica_groups=mesh['seq'=32,'dp'=8,'domain'=2] {'seq'}, dimensions={0}, use_global_device_ids=true | all-gather | bytes 135168 | tf_op jit(solution)/shard_map/all_gather | solution.py:15
  214.6 48.1 %all-gather.10.cloned.1.call-done = bf16[1024,1024]{1,0:T(8,128)(2,1)} async-done(((bf16[32,1024]{1,0:T(8,128)(2,1)}), bf16[1024,1024]{1,0:T(8,128)(2,1)}) %all-gather.10.cloned.1.call-update) | async-done | bytes 2097168 | tf_op jit(solution)/shard_map/all_gather | solution.py:62
  262.7 2.7 fusion.22
  265.4 0.0 copy-start.4
  265.4 0.5 select_reduce_fusion
  266.0 0.4 fusion.11
  266.3 145.7 %all-gather.14.cloned.1.call-done = f32[256,128,128]{2,1,0:T(8,128)} async-done(((f32[8,128,128]{2,1,0:T(8,128)}), f32[256,128,128]{2,1,0:T(8,128)}) %all-gather.14.cloned.1.call-update) | async-done | bytes 16777232 | tf_op jit(solution)/shard_map/all_gather | solution.py:15
  412.1 0.0 copy-done.4
  412.1 0.5 fusion.24
  412.6 1.4 fusion.21
  414.0 0.0 copy-start.1
  414.0 0.3 copy.47
  414.3 0.2 fusion.7
  414.6 65.2 %all-gather.1 = f32[32768]{0:T(1024)S(1)} all-gather(f32[1024]{0:T(1024)S(1)} %fusion.7), channel_id=3, replica_groups=mesh['seq'=32,'dp'=8,'domain'=2] {'seq'}, dimensions={0}, use_global_device_ids=true | all-gather | bytes 135168 | tf_op jit(solution)/shard_map/all_gather | solution.py:108
  479.8 0.6 multiply_reduce_fusion
  481.1 0.0 copy-done.1
  481.1 20.5 %all-gather.2 = bf16[8,1,1024]{2,1,0:T(2,128)(2,1)S(1)} all-gather(bf16[1,1,1024]{2,1,0:T(2,128)(2,1)S(1)} %bitcast.120), channel_id=1, replica_groups=mesh['seq'=32,'dp'=8,'domain'=2] {'dp'}, dimensions={0}, use_global_device_ids=true | all-gather | bytes 18432 | tf_op jit(solution)/shard_map/all_gather | solution.py:112
  501.7 18.0 %collective-permute-start = (bf16[8,1024]{1,0:T(8,128)(2,1)S(1)}, bf16[8,1024]{1,0:T(8,128)(2,1)S(1)}, u32[]{:S(2)}, u32[]{:S(2)}) collective-permute-start(bf16[8,1024]{1,0:T(8,128)(2,1)S(1)} %bitcast.119), channel_id=1, source_target_pairs={{0,1},{1,0},{2,3},{3,2},{4,5},{5,4},{6,7},{7,6},{8,9},{9,8},{10,11... | collective-permute-start | bytes 49160 | tf_op jit(solution)/shard_map/ppermute | solution.py:33
  519.7 0.6 dynamic-slice_bitcast_fusion
  520.3 0.2 collective-permute-done
  520.5 1.5 fusion.40
  (12 shorter events, 0.2 us)
Async XLA Ops:
  7.2 87.9 %all-gather.12.cloned.1.call-start = ((), (), s32[]{:S(2)}) async-start(), calls=%async_computation.2 | async-start | bytes 2162688 | tf_op jit(solution)/shard_map/all_gather | solution.py:63
  8.8 170.1 %all-gather.8.cloned.1.call-start = ((), (), s32[]{:S(2)}) async-start(), calls=%async_computation | async-start | bytes 2162688 | tf_op jit(solution)/shard_map/all_gather | solution.py:64
  9.6 253.1 %all-gather.10.cloned.1.call-start = ((), (), s32[]{:S(2)}) async-start(), calls=%async_computation.1 | async-start | bytes 2162688 | tf_op jit(solution)/shard_map/all_gather | solution.py:62
  10.3 401.7 %all-gather.14.cloned.1.call-start = ((), (), s32[]{:S(2)}) async-start(), calls=%async_computation.3 | async-start | bytes 17301504 | tf_op jit(solution)/shard_map/all_gather | solution.py:15
  95.1 83.8 %copy-start = (bf16[1,1,256,1024]{3,2,1,0:T(8,128)(2,1)S(1)}, bf16[1,1,256,1024]{3,2,1,0:T(8,128)(2,1)}, u32[]{:S(2)}) copy-start(bf16[1,1,256,1024]{3,2,1,0:T(8,128)(2,1)} %param.8) | copy-start | bytes 1572868
  95.1 83.8 %copy-start.2 = (f32[1,1024]{1,0:T(1,128)S(1)}, f32[1,1024]{1,0:T(1,128)}, u32[]{:S(2)}) copy-start(f32[1,1024]{1,0:T(1,128)} %param.10) | copy-start | bytes 12292
  98.3 84.1 %copy-start.3 = (s32[8]{0:T(128)S(1)}, s32[8]{0:T(128)}, u32[]{:S(2)}) copy-start(s32[8]{0:T(128)} %param.13) | copy-start | bytes 100
  265.4 146.6 %copy-start.4 = (bf16[32,8,8,128]{3,2,1,0:T(8,128)(2,1)}, bf16[32,8,8,128]{3,2,1,0:T(8,128)(2,1)S(1)}, u32[]{:S(2)}) copy-start(bf16[32,8,8,128]{3,2,1,0:T(8,128)(2,1)S(1)} %fusion.22) | copy-start | bytes 1572868
  414.0 67.1 %copy-start.1 = (f32[1,1024]{1,0:T(1,128)S(1)}, f32[1,1024]{1,0:T(1,128)}, u32[]{:S(2)}) copy-start(f32[1,1024]{1,0:T(1,128)} %param.11) | copy-start | bytes 12292
  501.7 18.8 %collective-permute-start = (bf16[8,1024]{1,0:T(8,128)(2,1)S(1)}, bf16[8,1024]{1,0:T(8,128)(2,1)S(1)}, u32[]{:S(2)}, u32[]{:S(2)}) collective-permute-start(bf16[8,1024]{1,0:T(8,128)(2,1)S(1)} %bitcast.119), channel_id=1, source_target_pairs={{0,1},{1,0},{2,3},{3,2},{4,5},{5,4},{6,7},{7,6},{8,9},{9,8},{10,11... | collective-permute-start | bytes 49160 | tf_op jit(solution)/shard_map/ppermute | solution.py:33
Sparse Core Ops, SparseCore 0:
  11.1 83.9 all-gather.11
  98.3 80.6 all-gather.7
  182.1 80.5 all-gather.9
  265.7 146.2 all-gather.13
